TPU v7x, 32 devices: a whole 2x2x4 slice. The times are simulated.
32 devices in a mesh: seq: 4 (over y, x), hv: 8 (over z, core).
Axes of the slice: x: 2, y: 2, z: 4, core: 2. Of those that a mesh axis runs over, the one named last changes fastest.
Arguments:
- qproj: bfloat16 [8192, 2048], P(('seq', 'hv')), may hold values from -6 to 6
- kproj: bfloat16 [8192, 2048], P(('seq', 'hv')), may hold values from -6 to 6
- vproj: bfloat16 [8192, 4096], P(('seq', 'hv')), may hold values from -40 to 40
- igate: bfloat16 [8192, 8], P(('seq', 'hv')), may hold values from -10 to 10
- fgate: bfloat16 [8192, 8], P(('seq', 'hv')), may hold values from -0.1 to 24
- ogate: bfloat16 [8192, 4096], P(('seq', 'hv')), may hold values from -8 to 8
- norm_gain: bfloat16 [4096], replicated, may hold values from 0.099609375 to 1.8984375
Outputs:
- gated: bfloat16 [8192, 4096], P(('seq', 'hv'))
All inputs are finite; a program needn't handle non-finite values.
Results may differ from a plain program's by a relative error of at most 0.0052.
Values may be sent and summed in bfloat16 or wider, within the bound.
No kernel may reach another device: no remote copies, remote signals or barrier semaphores. Data moves between devices by JAX's collectives and lax.ppermute only.
A program may use at most 64 MiB of HBM per device.

v0:
```python
import functools
import math

import jax
import jax.numpy as jnp
from jax import lax
from jax.experimental import pallas as pl
from jax.experimental.pallas import tpu as pltpu
from jax.sharding import Mesh
from jax.sharding import PartitionSpec as P


F32 = jnp.float32
BF16 = jnp.bfloat16
CORES = 2
PAD = 8
PIECES = 3
CHUNKS = 2


def call(kernel, outs, ins, scratch=()):
    vmem = pl.BlockSpec(memory_space=pltpu.VMEM)
    return pl.pallas_call(
        kernel,
        out_shape=outs,
        in_specs=[vmem] * len(ins),
        out_specs=[vmem] * len(outs),
        scratch_shapes=list(scratch),
        compiler_params=pltpu.CompilerParams(vmem_limit_bytes=8 << 20),
    )(*ins)


def shape(dims, dtype):
    return jax.ShapeDtypeStruct(dims, dtype)


def rows_at(start, size):
    return pl.ds(pl.multiple_of(start, size), size)


def head_cols(j, half, width):
    head = lax.rem(lax.axis_index("core") * half + j, CORES * half)
    return pl.ds(pl.multiple_of(head * width, width), width)


def first_kernel(ig, fg, q, k, v, rowa, cols, out, core, qv, kv, vv, igv, fgv, sems, *, scale, first, per):
    def block(source, target, i):
        width = source.shape[1] // (2 * first // per)
        at = lax.rem(lax.axis_index("core") * (first // per) + i, 2 * first // per)
        at = pl.ds(pl.multiple_of(at * width, width), width)
        return source.at[:, at], target.at[:, at]

    blocks = [first // per] + [i for i in range(2 * first // per) if i != first // per]
    sources = [(fg, fgv), (ig, igv)] + [block(*a, i) for i in blocks for a in ((k, kv), (v, vv))] + [(q, qv)]
    moves = [pltpu.make_async_copy(*pair, sems.at[i]) for i, pair in enumerate(sources)]
    for move in moves:
        move.start()
    heads, tok = igv.shape
    half = heads // CORES
    zero = lax.axis_index("core") == 0
    core[0] = lax.axis_index("core").astype(jnp.int32)
    earlier = lax.broadcasted_iota(jnp.int32, (tok, tok), 0)
    later = lax.broadcasted_iota(jnp.int32, (tok, tok), 1)
    tri = (earlier <= later).astype(F32).astype(BF16)
    own_first = lambda a: jnp.where(zero, a, jnp.concatenate([a[half:], a[:half]], axis=0))
    moves[0].wait()
    lf = own_first(jax.nn.log_sigmoid(fgv[...].astype(F32)))
    high = lf.astype(BF16)
    rest = lf - high.astype(F32)
    mid = rest.astype(BF16)
    low = (rest - mid.astype(F32)).astype(BF16)
    sums = lambda a: jnp.dot(a, tri, preferred_element_type=F32)
    g = sums(high) + sums(mid) + sums(low)
    last = g[:, tok - 1 : tok]
    moves[1].wait()
    il = own_first(15.0 * jnp.tanh(igv[...].astype(F32) / 15.0))
    rowa[...] = il - g
    cols[...] = jnp.concatenate([g, jnp.exp(last - g + il), jnp.exp(g) / scale], axis=0).T
    size = out.shape[0] - heads
    out[size:, :] = jnp.broadcast_to(last, (heads, out.shape[1]))
    moves[2].wait()
    moves[3].wait()
    state_body(kv, vv, cols, out, first=first, per=per, half=half, dkey=size // per)
    for move in moves[4:]:
        move.wait()


def state_body(k, v, cols, out, *, first, per, half, dkey):
    heads, dval = CORES * half, out.shape[1]
    dims = (((0,), (0,)), ((), ()))
    for j in range(per):
        weight = cols[:, heads + first + j : heads + first + j + 1]
        kw = k[:, head_cols(first + j, half, dkey)].astype(F32) * weight
        high = kw.astype(BF16)
        low = (kw - high.astype(F32)).astype(BF16)
        value = v[:, head_cols(first + j, half, dval)]
        part = lax.dot_general(high, value, dims, preferred_element_type=F32)
        out[j * dkey : (j + 1) * dkey, :] = part + lax.dot_general(low, value, dims, preferred_element_type=F32)


def state_kernel(k, v, cols, out, *, first, per, half):
    state_body(k, v, cols, out, first=first, per=per, half=half, dkey=out.shape[0] // per)


def put_logs(ref, start, values):
    rows = lax.broadcasted_iota(jnp.int32, (PAD, ref.shape[1]), 0)
    tile = jnp.zeros((PAD, ref.shape[1]), F32)
    for i, value in enumerate(values):
        high = value.astype(BF16).astype(F32)
        mid = (value - high).astype(BF16).astype(F32)
        for j, piece in enumerate((high, mid, value - high - mid)):
            tile = jnp.where(rows == PIECES * i + j, piece, tile)
    ref[start:, :] = tile.astype(BF16)


def get_log(ref, start, i):
    tile = ref[start:, :].astype(F32)
    rows = [tile[j : j + 1] for j in range(PIECES * i, PIECES * i + PIECES)]
    return rows[0] + rows[1] + rows[2]


def chip_kernel(own, rec, table, rtable, *msgs, chunk, per, half, dkey, rows):
    place, zero = lax.axis_index("z"), lax.axis_index("core") == 0
    base = table.shape[0] - CORES * half
    for k in range(len(msgs)):
        dest = place ^ k
        here = rows_at(dest * rows, rows)
        head = base + (dest * rows) // dkey
        logs = [
            (table[pl.ds(head + i * per, 1), :], rtable[pl.ds(head + i * per + half, 1), :]) for i in range(CHUNKS)
        ]
        ga, gb = logs[chunk]
        decay = jnp.exp(jnp.where(zero, gb, ga))
        a, b = own[here, :], rec[here, :]
        state = decay * jnp.where(zero, a, b) + jnp.where(zero, b, a)
        msgs[k][0:rows, :] = state.astype(BF16)
        if chunk == 0:
            put_logs(msgs[k], rows, [x + y for x, y in logs])


def column_kernel(*refs, rows, nz, chunk):
    msgs, heads, out = refs[:nz], refs[-1 - nz : -1], refs[-1]
    place = lax.axis_index("z")
    logs = [[get_log(m, rows, i) for m in heads] for i in (range(CHUNKS) if chunk == 0 else [chunk])]
    own = logs[0]
    places = [place ^ k for k in range(nz)]
    total = jnp.zeros((rows, out.shape[1]), F32)
    for k in range(nz):
        behind = jnp.zeros_like(own[0])
        for j in range(nz):
            if j != k:
                behind = behind + jnp.where(places[j] > places[k], own[j], 0.0)
        total = total + jnp.exp(behind) * msgs[k][0:rows, :].astype(F32)
    out[0:rows, :] = total.astype(BF16)
    if chunk == 0:
        put_logs(out, rows, [functools.reduce(lambda x, y: x + y, log) for log in logs])


def prefix_kernel(*refs, rows, nz, spans, chunk):
    count = nz + spans - 1
    msgs, cols = refs[:nz], refs[nz:count]
    if chunk:
        heads, rheads, refs = refs[count : count + nz], refs[count + nz : 2 * count], refs[2 * count :]
    else:
        heads, rheads, refs = msgs, cols, refs[count:]
    outs = refs[:nz]
    states, logs, pres = refs[nz:]
    place, span = lax.axis_index("z"), lax.axis_index("seq")
    for k in range(nz):
        states[place ^ k] = msgs[k][0:rows, :].astype(F32)
        logs[place ^ k] = jnp.broadcast_to(get_log(heads[k], rows, chunk), logs.shape[1:])
    state = jnp.zeros(states.shape[1:], F32)
    earlier = [span ^ k for k in range(1, spans)]
    decays = [jnp.where(s < span, get_log(head, rows, chunk), 0.0) for s, head in zip(earlier, rheads)]
    for s, col in zip(earlier, cols):
        behind = jnp.zeros_like(decays[0])
        for t, decay in zip(earlier, decays):
            behind = behind + jnp.where(t > s, decay, 0.0)
        state = state + jnp.where(s < span, jnp.exp(behind) * col[0:rows, :].astype(F32), 0.0)
    for z in range(nz):
        pres[z] = state.astype(BF16)
        state = jnp.exp(logs[z][0:1, :]) * state + states[z]
    for k in range(nz):
        outs[k][...] = pres[place ^ k]


def spread_kernel(*refs, first, half, dkey, rows, nz):
    parts = refs[:nz]
    own, rec, table, rtable, mine, other = refs[nz:]
    place, zero = lax.axis_index("z"), lax.axis_index("core") == 0
    base = table.shape[0] - CORES * half
    for k in range(nz):
        source = place ^ k
        here = rows_at(source * rows, rows)
        head = base + first + (source * rows) // dkey
        decay = jnp.exp(jnp.where(zero, table[pl.ds(head, 1), :], rtable[pl.ds(head + half, 1), :]))
        before = parts[k][...].astype(F32)
        behind = decay * before + jnp.where(zero, own[here, :], rec[here, :])
        mine[here, :] = jnp.where(zero, before, behind).astype(BF16)
        other[here, :] = jnp.where(zero, behind, before).astype(BF16)


def gate_kernel(og, gain, out, *, half, dval):
    for j in range(CORES * half):
        at = head_cols(j, half, dval)
        out[:, j * dval : (j + 1) * dval] = gain[:, at].astype(F32) * jax.nn.sigmoid(og[:, at].astype(F32))


def intra_kernel(q, k, v, rowa, cols, out, *, half, dkey, dval, scale):
    tok = q.shape[0]
    rows = lax.broadcasted_iota(jnp.int32, (tok, tok), 0)
    lanes = lax.broadcasted_iota(jnp.int32, (tok, tok), 1)
    causal = lanes <= rows
    for j in range(CORES * half):
        at = head_cols(j, half, dkey)
        scores = lax.dot_general(q[:, at], k[:, at], (((1,), (1,)), ((), ())), preferred_element_type=F32)
        logw = jnp.where(causal, cols[:, j : j + 1] + rowa[j : j + 1, :], -jnp.inf)
        prod = (scores / scale * jnp.exp(logw)).astype(BF16)
        out[:, j * dval : (j + 1) * dval] = jnp.dot(
            prod, v[:, head_cols(j, half, dval)], preferred_element_type=F32
        )


def final_kernel(core, q, state, intra, cols, gate, *rest, first, per, half):
    out = rest[-1]
    heads = CORES * half
    dkey, dval = state.shape[0] // per, state.shape[1]
    for j in range(per):
        head = first + j
        here = slice(head * dval, (head + 1) * dval)
        inter = jnp.dot(
            q[:, head_cols(head, half, dkey)], state[j * dkey : (j + 1) * dkey, :], preferred_element_type=F32
        )
        decay = cols[:, 2 * heads + head : 2 * heads + head + 1]
        hval = (intra[:, here] + decay * inter).astype(BF16).astype(F32)
        meansq = jnp.mean(hval * hval, axis=1, keepdims=True)
        normed = hval * lax.rsqrt(meansq + 1e-06)
        out[:, j * dval : (j + 1) * dval] = (normed * gate[:, here]).astype(BF16)


def final(core, q, state, intra, cols, gate, out, *, first, per, half, dval):
    tok = q.shape[0]
    blocks = CORES * half // per
    at = lambda j, s: (0, lax.rem(s[0] * (half // per) + first // per, blocks))
    vmem = pl.BlockSpec(memory_space=pltpu.VMEM)
    ins = [q, state, intra, cols, gate]
    specs = [vmem] * len(ins)
    aliases = {}
    if out is not None:
        ins.append(out)
        specs.append(pl.BlockSpec(memory_space=pl.ANY))
        aliases = {len(ins): 0}
    return pl.pallas_call(
        functools.partial(final_kernel, first=first, per=per, half=half),
        out_shape=shape((tok, CORES * half * dval), BF16),
        grid_spec=pltpu.PrefetchScalarGridSpec(
            num_scalar_prefetch=1,
            grid=(1,),
            in_specs=specs,
            out_specs=pl.BlockSpec((tok, per * dval), at),
        ),
        input_output_aliases=aliases,
        compiler_params=pltpu.CompilerParams(vmem_limit_bytes=8 << 20),
    )(core, *ins)


def after(value, *others):
    return lax.optimization_barrier((value,) + others)[0]


def shards(qproj, kproj, vproj, igate, fgate, ogate, norm_gain):
    spans, nz = lax.axis_size("seq"), lax.axis_size("z")
    tok, heads = igate.shape
    dkey = qproj.shape[1] // heads
    dval = vproj.shape[1] // heads
    half = heads // CORES
    per = half // CHUNKS
    rows = per * dkey // nz
    assert rows % PAD == 0 and dkey % rows == 0 and PIECES * CHUNKS <= PAD
    assert nz & (nz - 1) == 0 and spans & (spans - 1) == 0
    scale = math.sqrt(dkey)

    def swap(a, axis, bit, up=False):
        pairs = [(j, j ^ bit) for j in range(lax.axis_size(axis)) if not up or j < j ^ bit]
        return lax.ppermute(a, axis, pairs)

    vmem, hbm = pl.BlockSpec(memory_space=pltpu.VMEM), pl.BlockSpec(memory_space=pltpu.HBM)
    loads = [shape(qproj.shape, BF16), shape(kproj.shape, BF16), shape(vproj.shape, BF16)]
    rowa, cols, table, core, qvm, kvm, vvm = pl.pallas_call(
        functools.partial(first_kernel, scale=scale, first=half, per=per),
        out_shape=[
            shape((heads, tok), F32),
            shape((tok, 3 * heads), F32),
            shape((per * dkey + heads, dval), F32),
            shape((1,), jnp.int32),
        ] + loads,
        in_specs=[hbm] * 5,
        out_specs=[vmem, vmem, vmem, pl.BlockSpec(memory_space=pltpu.SMEM), vmem, vmem, vmem],
        scratch_shapes=[
            pltpu.VMEM((heads, tok), BF16),
            pltpu.VMEM((heads, tok), BF16),
            pltpu.SemaphoreType.DMA((3 + 2 * CORES * CHUNKS,)),
        ],
        compiler_params=pltpu.CompilerParams(vmem_limit_bytes=8 << 20),
        name="first",
    )(*(pltpu.with_memory_space_constraint(a, pltpu.HBM) for a in (igate.T, fgate.T, qproj, kproj, vproj)))

    def state(first):
        return call(
            functools.partial(state_kernel, first=first, per=per, half=half),
            [shape((per * dkey, dval), F32)],
            [kvm, vvm, cols],
        )[0]

    others = [table] + [state(half + i * per) for i in range(1, CHUNKS)]
    recs = [swap(other, "core", 1) for other in others]
    owns = [state(i * per) for i in range(CHUNKS)]
    rtable = recs[0]

    pads = [PAD] + [0] * (CHUNKS - 1)
    sent = []
    for i in range(CHUNKS):
        msgs = call(
            functools.partial(chip_kernel, chunk=i, per=per, half=half, dkey=dkey, rows=rows),
            [shape((rows + pads[i], dval), BF16)] * nz,
            [owns[i], recs[i], table, rtable],
        )
        sent.append([msgs[0]] + [swap(msgs[k], "z", k) for k in range(1, nz)])

    gate = call(
        functools.partial(gate_kernel, half=half, dval=dval),
        [shape((tok, heads * dval), F32)],
        [ogate, norm_gain.reshape(1, heads * dval)],
    )[0]
    intra = call(
        functools.partial(intra_kernel, half=half, dkey=dkey, dval=dval, scale=scale),
        [shape((tok, heads * dval), F32)],
        [qvm, kvm, vvm, rowa, after(cols, sent[-1][0])],
    )[0]
    sent[0][0] = after(sent[0][0], intra, gate)

    parts, cumuls = [], []
    for i in range(CHUNKS):
        total = call(
            functools.partial(column_kernel, rows=rows, nz=nz, chunk=i),
            [shape((rows + pads[i], dval), BF16)],
            sent[i] + (sent[0] if i else []),
        )[0]
        cumuls.append([swap(total, "seq", k, up=True) for k in range(1, spans)])
        pres = call(
            functools.partial(prefix_kernel, rows=rows, nz=nz, spans=spans, chunk=i),
            [shape((rows, dval), BF16)] * nz,
            sent[i] + cumuls[i] + (sent[0] + cumuls[0] if i else []),
            [
                pltpu.VMEM((nz, rows, dval), F32),
                pltpu.VMEM((nz, 8, dval), F32),
                pltpu.VMEM((nz, rows, dval), BF16),
            ],
        )
        parts.append([pres[0]] + [swap(pres[k], "z", k) for k in range(1, nz)])
    out = None
    for i in range(CHUNKS):
        own = owns[i] if out is None else after(owns[i], out)
        mine, other = call(
            functools.partial(spread_kernel, first=i * per, half=half, dkey=dkey, rows=rows, nz=nz),
            [shape((per * dkey, dval), BF16)] * 2,
            parts[i] + [own, recs[i], table, rtable],
        )
        back = swap(other, "core", 1)
        for where, memory in ((i * per, mine), (half + i * per, back)):
            out = final(
                core, qvm, memory, intra, cols, gate, out,
                first=where, per=per, half=half, dval=dval,
            )
    return out


def solution(mesh):
    spans, lanes = mesh.shape["seq"], mesh.shape["hv"]
    nz = lanes // CORES
    inner = Mesh(mesh.devices.reshape(spans, nz, CORES), ("seq", "z", "core"))
    split = P(("seq", "z", "core"), None)

    return jax.shard_map(shards, mesh=inner, in_specs=(split,) * 6 + (P(),), out_specs=split, check_vma=False)
```

profile of v0, /device:TPU:21, one launch (start us, length us, event | category | flops | bytes accessed | tf_op | source)
XLA Modules:
  0.0 94.2 jit_solution(14870039850290939261)
XLA Ops:
  0.0 2.8 %first.1 = (f32[8,256]{1,0:T(8,128)S(1)}, f32[256,24]{1,0:T(8,128)S(1)}, f32[520,512]{1,0:T(8,128)S(1)}, s32[1]{0:T(128)}, bf16[256,2048]{1,0:T(8,128)(2,1)S(1)}...) custom-call(bf16[8,256]{1,0:T(8,128)(2,1)} %bitcast.2, bf16[8,256]{1,0:T(8,128)(2,1)} %bitcast.3, ...), custom_call_target="tpu_custom_call" | custom-call | tf_op jit(solution)/shard_map/first/pallas_call | solution.py:289
  6.2 1.4 %collective-permute-start.5 = (bf16[136,512]{1,0:T(8,128)(2,1)S(1)}, bf16[136,512]{1,0:T(8,128)(2,1)S(1)}, u32[]{:S(2)}, u32[]{:S(2)}) collective-permute-start(bf16[136,512]{1,0:T(8,128)(2,1)S(1)} %get-tuple-element.49), channel_id=1, source_target_pairs={{0,2},{2,0},{4,6},{6,4},{1,3},{3,1},{5,7},{7,5},{8,10},{10,8},{12,... | collective-permute-start | bytes 417800 | tf_op jit(solution)/shard_map/ppermute | solution.py:285
  7.6 1.3 %collective-permute-start.7 = (bf16[136,512]{1,0:T(8,128)(2,1)S(1)}, bf16[136,512]{1,0:T(8,128)(2,1)S(1)}, u32[]{:S(2)}, u32[]{:S(2)}) collective-permute-start(bf16[136,512]{1,0:T(8,128)(2,1)S(1)} %get-tuple-element.51), channel_id=1, source_target_pairs={{0,6},{2,4},{4,2},{6,0},{1,7},{3,5},{5,3},{7,1},{8,14},{10,12},{12... | collective-permute-start | bytes 417800 | tf_op jit(solution)/shard_map/ppermute | solution.py:285
  10.3 1.8 %shard_map.78.intra = f32[256,4096]{1,0:T(8,128)S(1)} custom-call(bf16[256,2048]{1,0:T(8,128)(2,1)S(1)} %get-tuple-element.36.q, bf16[256,2048]{1,0:T(8,128)(2,1)S(1)} %get-tuple-element.37.k, bf16[256,4096]{1,0:T(8,128)(2,1)S(1)} %get-tuple-element.38.v, f32[8,256]{1,0:T(8,128)S(1)} %get-tuple-element.46.rowa, f32[256,24]{1,0:T(8,128)S(1)} %get-tuple-element.47.cols), custom_call_target="tpu_custom_call" | custom-call | tf_op jit(solution)/shard_map/pallas_call | solution.py:23
  12.1 2.0 %collective-permute-done.6.refs_6_.refs_2_.refs_9_ = bf16[136,512]{1,0:T(8,128)(2,1)S(1)} collective-permute-done((bf16[136,512]{1,0:T(8,128)(2,1)S(1)}, bf16[136,512]{1,0:T(8,128)(2,1)S(1)}, u32[]{:S(2)}, u32[]{:S(2)}) %collective-permute-start.6) | collective-permute-done | bytes 139296 | tf_op jit(solution)/shard_map/ppermute | solution.py:285
  14.2 6.9 %collective-permute-done.7.refs_7_.refs_3_.refs_10_ = bf16[136,512]{1,0:T(8,128)(2,1)S(1)} collective-permute-done((bf16[136,512]{1,0:T(8,128)(2,1)S(1)}, bf16[136,512]{1,0:T(8,128)(2,1)S(1)}, u32[]{:S(2)}, u32[]{:S(2)}) %collective-permute-start.7) | collective-permute-done | bytes 139296 | tf_op jit(solution)/shard_map/ppermute | solution.py:285
  21.2 3.1 %collective-permute-start.11 = (bf16[136,512]{1,0:T(8,128)(2,1)S(1)}, bf16[136,512]{1,0:T(8,128)(2,1)S(1)}, u32[]{:S(2)}, u32[]{:S(2)}) collective-permute-start(bf16[136,512]{1,0:T(8,128)(2,1)S(1)} %shard_map.81), channel_id=1, source_target_pairs={{0,8},{16,24},{1,9},{17,25},{2,10},{18,26},{3,11},{19,27},{4,12},{... | collective-permute-start | bytes 417800 | tf_op jit(solution)/shard_map/ppermute | solution.py:285
  24.4 1.3 %collective-permute-start.12 = (bf16[136,512]{1,0:T(8,128)(2,1)S(1)}, bf16[136,512]{1,0:T(8,128)(2,1)S(1)}, u32[]{:S(2)}, u32[]{:S(2)}) collective-permute-start(bf16[136,512]{1,0:T(8,128)(2,1)S(1)} %shard_map.81), channel_id=1, source_target_pairs={{0,16},{8,24},{1,17},{9,25},{2,18},{10,26},{3,19},{11,27},{4,20},{... | collective-permute-start | bytes 417800 | tf_op jit(solution)/shard_map/ppermute | solution.py:285
  25.7 1.3 %collective-permute-start.13 = (bf16[136,512]{1,0:T(8,128)(2,1)S(1)}, bf16[136,512]{1,0:T(8,128)(2,1)S(1)}, u32[]{:S(2)}, u32[]{:S(2)}) collective-permute-start(bf16[136,512]{1,0:T(8,128)(2,1)S(1)} %shard_map.81), channel_id=1, source_target_pairs={{0,24},{8,16},{1,25},{9,17},{2,26},{10,18},{3,27},{11,19},{4,28},{... | collective-permute-start | bytes 417800 | tf_op jit(solution)/shard_map/ppermute | solution.py:285
  27.0 3.2 %collective-permute-done.12.refs_12_.refs_5_ = bf16[136,512]{1,0:T(8,128)(2,1)S(1)} collective-permute-done((bf16[136,512]{1,0:T(8,128)(2,1)S(1)}, bf16[136,512]{1,0:T(8,128)(2,1)S(1)}, u32[]{:S(2)}, u32[]{:S(2)}) %collective-permute-start.12) | collective-permute-done | bytes 139296 | tf_op jit(solution)/shard_map/ppermute | solution.py:285
  30.2 2.3 %collective-permute-done.13.refs_13_.refs_6_ = bf16[136,512]{1,0:T(8,128)(2,1)S(1)} collective-permute-done((bf16[136,512]{1,0:T(8,128)(2,1)S(1)}, bf16[136,512]{1,0:T(8,128)(2,1)S(1)}, u32[]{:S(2)}, u32[]{:S(2)}) %collective-permute-start.13) | collective-permute-done | bytes 139296 | tf_op jit(solution)/shard_map/ppermute | solution.py:285
  34.2 1.3 %collective-permute-start.19 = (bf16[128,512]{1,0:T(8,128)(2,1)S(1)}, bf16[128,512]{1,0:T(8,128)(2,1)S(1)}, u32[]{:S(2)}, u32[]{:S(2)}) collective-permute-start(bf16[128,512]{1,0:T(8,128)(2,1)S(1)} %get-tuple-element.59), channel_id=1, source_target_pairs={{0,6},{2,4},{4,2},{6,0},{1,7},{3,5},{5,3},{7,1},{8,14},{10,12},{12... | collective-permute-start | bytes 393224 | tf_op jit(solution)/shard_map/ppermute | solution.py:285
  36.7 1.3 %collective-permute-done.18.refs_2_ = bf16[128,512]{1,0:T(8,128)(2,1)S(1)} collective-permute-done((bf16[128,512]{1,0:T(8,128)(2,1)S(1)}, bf16[128,512]{1,0:T(8,128)(2,1)S(1)}, u32[]{:S(2)}, u32[]{:S(2)}) %collective-permute-start.18) | collective-permute-done | bytes 131104 | tf_op jit(solution)/shard_map/ppermute | solution.py:285
  38.1 8.3 %collective-permute-done.19.refs_3_ = bf16[128,512]{1,0:T(8,128)(2,1)S(1)} collective-permute-done((bf16[128,512]{1,0:T(8,128)(2,1)S(1)}, bf16[128,512]{1,0:T(8,128)(2,1)S(1)}, u32[]{:S(2)}, u32[]{:S(2)}) %collective-permute-start.19) | collective-permute-done | bytes 131104 | tf_op jit(solution)/shard_map/ppermute | solution.py:285
  46.9 2.2 %collective-permute-start.20 = (bf16[512,512]{1,0:T(8,128)(2,1)S(1)}, bf16[512,512]{1,0:T(8,128)(2,1)S(1)}, u32[]{:S(2)}, u32[]{:S(2)}) collective-permute-start(bf16[512,512]{1,0:T(8,128)(2,1)S(1)} %get-tuple-element.60), channel_id=1, source_target_pairs={{0,1},{1,0},{2,3},{3,2},{4,5},{5,4},{6,7},{7,6},{8,9},{9,8},{10,11... | collective-permute-start | bytes 1572872 | tf_op jit(solution)/shard_map/ppermute | solution.py:285
  50.3 1.4 %collective-permute-start.4 = (bf16[128,512]{1,0:T(8,128)(2,1)S(1)}, bf16[128,512]{1,0:T(8,128)(2,1)S(1)}, u32[]{:S(2)}, u32[]{:S(2)}) collective-permute-start(bf16[128,512]{1,0:T(8,128)(2,1)S(1)} %get-tuple-element.44), channel_id=1, source_target_pairs={{0,6},{2,4},{4,2},{6,0},{1,7},{3,5},{5,3},{7,1},{8,14},{10,12},{12... | collective-permute-start | bytes 393224 | tf_op jit(solution)/shard_map/ppermute | solution.py:285
  51.7 2.3 %collective-permute-done.2.refs_1_ = bf16[128,512]{1,0:T(8,128)(2,1)S(1)} collective-permute-done((bf16[128,512]{1,0:T(8,128)(2,1)S(1)}, bf16[128,512]{1,0:T(8,128)(2,1)S(1)}, u32[]{:S(2)}, u32[]{:S(2)}) %collective-permute-start.2) | collective-permute-done | bytes 131104 | tf_op jit(solution)/shard_map/ppermute | solution.py:285
  54.0 2.6 %collective-permute-done.3.refs_2_ = bf16[128,512]{1,0:T(8,128)(2,1)S(1)} collective-permute-done((bf16[128,512]{1,0:T(8,128)(2,1)S(1)}, bf16[128,512]{1,0:T(8,128)(2,1)S(1)}, u32[]{:S(2)}, u32[]{:S(2)}) %collective-permute-start.3) | collective-permute-done | bytes 131104 | tf_op jit(solution)/shard_map/ppermute | solution.py:285
  56.7 6.7 %collective-permute-done.4.refs_3_ = bf16[128,512]{1,0:T(8,128)(2,1)S(1)} collective-permute-done((bf16[128,512]{1,0:T(8,128)(2,1)S(1)}, bf16[128,512]{1,0:T(8,128)(2,1)S(1)}, u32[]{:S(2)}, u32[]{:S(2)}) %collective-permute-start.4) | collective-permute-done | bytes 131104 | tf_op jit(solution)/shard_map/ppermute | solution.py:285
  63.5 2.2 %collective-permute-start.8 = (bf16[128,512]{1,0:T(8,128)(2,1)S(1)}, bf16[128,512]{1,0:T(8,128)(2,1)S(1)}, u32[]{:S(2)}, u32[]{:S(2)}) collective-permute-start(bf16[128,512]{1,0:T(8,128)(2,1)S(1)} %shard_map.80), channel_id=1, source_target_pairs={{0,8},{16,24},{1,9},{17,25},{2,10},{18,26},{3,11},{19,27},{4,12},{... | collective-permute-start | bytes 393224 | tf_op jit(solution)/shard_map/ppermute | solution.py:285
  65.7 1.3 %collective-permute-start.9 = (bf16[128,512]{1,0:T(8,128)(2,1)S(1)}, bf16[128,512]{1,0:T(8,128)(2,1)S(1)}, u32[]{:S(2)}, u32[]{:S(2)}) collective-permute-start(bf16[128,512]{1,0:T(8,128)(2,1)S(1)} %shard_map.80), channel_id=1, source_target_pairs={{0,16},{8,24},{1,17},{9,25},{2,18},{10,26},{3,19},{11,27},{4,20},{... | collective-permute-start | bytes 393224 | tf_op jit(solution)/shard_map/ppermute | solution.py:285
  67.0 1.3 %collective-permute-start.10 = (bf16[128,512]{1,0:T(8,128)(2,1)S(1)}, bf16[128,512]{1,0:T(8,128)(2,1)S(1)}, u32[]{:S(2)}, u32[]{:S(2)}) collective-permute-start(bf16[128,512]{1,0:T(8,128)(2,1)S(1)} %shard_map.80), channel_id=1, source_target_pairs={{0,24},{8,16},{1,25},{9,17},{2,26},{10,18},{3,27},{11,19},{4,28},{... | collective-permute-start | bytes 393224 | tf_op jit(solution)/shard_map/ppermute | solution.py:285
  68.3 3.1 %collective-permute-done.9.refs_5_ = bf16[128,512]{1,0:T(8,128)(2,1)S(1)} collective-permute-done((bf16[128,512]{1,0:T(8,128)(2,1)S(1)}, bf16[128,512]{1,0:T(8,128)(2,1)S(1)}, u32[]{:S(2)}, u32[]{:S(2)}) %collective-permute-start.9) | collective-permute-done | bytes 131104 | tf_op jit(solution)/shard_map/ppermute | solution.py:285
  71.4 2.3 %collective-permute-done.10.refs_6_ = bf16[128,512]{1,0:T(8,128)(2,1)S(1)} collective-permute-done((bf16[128,512]{1,0:T(8,128)(2,1)S(1)}, bf16[128,512]{1,0:T(8,128)(2,1)S(1)}, u32[]{:S(2)}, u32[]{:S(2)}) %collective-permute-start.10) | collective-permute-done | bytes 131104 | tf_op jit(solution)/shard_map/ppermute | solution.py:285
  74.2 1.3 %collective-permute-start.15 = (bf16[128,512]{1,0:T(8,128)(2,1)S(1)}, bf16[128,512]{1,0:T(8,128)(2,1)S(1)}, u32[]{:S(2)}, u32[]{:S(2)}) collective-permute-start(bf16[128,512]{1,0:T(8,128)(2,1)S(1)} %get-tuple-element.54), channel_id=1, source_target_pairs={{0,4},{2,6},{4,0},{6,2},{1,5},{3,7},{5,1},{7,3},{8,12},{10,14},{12... | collective-permute-start | bytes 393224 | tf_op jit(solution)/shard_map/ppermute | solution.py:285
  75.5 1.3 %collective-permute-start.16 = (bf16[128,512]{1,0:T(8,128)(2,1)S(1)}, bf16[128,512]{1,0:T(8,128)(2,1)S(1)}, u32[]{:S(2)}, u32[]{:S(2)}) collective-permute-start(bf16[128,512]{1,0:T(8,128)(2,1)S(1)} %get-tuple-element.55), channel_id=1, source_target_pairs={{0,6},{2,4},{4,2},{6,0},{1,7},{3,5},{5,3},{7,1},{8,14},{10,12},{12... | collective-permute-start | bytes 393224 | tf_op jit(solution)/shard_map/ppermute | solution.py:285
  76.8 1.9 %shard_map.85.rest_0_ = bf16[256,4096]{1,0:T(8,128)(2,1)} custom-call(s32[1]{0:T(128)} %get-tuple-element.35.core, bf16[256,2048]{1,0:T(8,128)(2,1)S(1)} %get-tuple-element.36.q, bf16[512,512]{1,0:T(8,128)(2,1)S(1)} %get-tuple-element.61.state, f32[256,4096]{1,0:T(8,128)S(1)} %shard_map.78.intra, f32[256,24]{1,0:T(8,128)S(1)} %get-tuple-element.47.cols, ...), custom_call_target="tpu_custom_call" | custom-call | tf_op jit(solution)/shard_map/pallas_call | solution.py:253
  78.7 1.9 %shard_map.86.rest_0_ = bf16[256,4096]{1,0:T(8,128)(2,1)} custom-call(s32[1]{0:T(128)} %get-tuple-element.35.core, bf16[256,2048]{1,0:T(8,128)(2,1)S(1)} %get-tuple-element.36.q, bf16[512,512]{1,0:T(8,128)(2,1)S(1)} %collective-permute-done.20.state, f32[256,4096]{1,0:T(8,128)S(1)} %shard_map.78.intra, ...), custom_call_target="tpu_custom_call", output_to_operand_aliasing={{}: (6, {})} | custom-call | tf_op jit(solution)/shard_map/pallas_call | solution.py:253
  80.7 7.6 %collective-permute-done.16.refs_3_ = bf16[128,512]{1,0:T(8,128)(2,1)S(1)} collective-permute-done((bf16[128,512]{1,0:T(8,128)(2,1)S(1)}, bf16[128,512]{1,0:T(8,128)(2,1)S(1)}, u32[]{:S(2)}, u32[]{:S(2)}) %collective-permute-start.16) | collective-permute-done | bytes 131104 | tf_op jit(solution)/shard_map/ppermute | solution.py:285
  88.8 1.5 %collective-permute-start.21 = (bf16[512,512]{1,0:T(8,128)(2,1)S(1)}, bf16[512,512]{1,0:T(8,128)(2,1)S(1)}, u32[]{:S(2)}, u32[]{:S(2)}) collective-permute-start(bf16[512,512]{1,0:T(8,128)(2,1)S(1)} %get-tuple-element.63), channel_id=1, source_target_pairs={{0,1},{1,0},{2,3},{3,2},{4,5},{5,4},{6,7},{7,6},{8,9},{9,8},{10,11... | collective-permute-start | bytes 1572872 | tf_op jit(solution)/shard_map/ppermute | solution.py:285
  90.3 1.9 %shard_map.88.rest_0_ = bf16[256,4096]{1,0:T(8,128)(2,1)} custom-call(s32[1]{0:T(128)} %get-tuple-element.35.core, bf16[256,2048]{1,0:T(8,128)(2,1)S(1)} %get-tuple-element.36.q, bf16[512,512]{1,0:T(8,128)(2,1)S(1)} %get-tuple-element.64.state, f32[256,4096]{1,0:T(8,128)S(1)} %shard_map.78.intra, ...), custom_call_target="tpu_custom_call", output_to_operand_aliasing={{}: (6, {})} | custom-call | tf_op jit(solution)/shard_map/pallas_call | solution.py:253
  92.3 1.9 %shard_map.89 = bf16[256,4096]{1,0:T(8,128)(2,1)} custom-call(s32[1]{0:T(128)} %get-tuple-element.35.core, bf16[256,2048]{1,0:T(8,128)(2,1)S(1)} %get-tuple-element.36.q, bf16[512,512]{1,0:T(8,128)(2,1)S(1)} %collective-permute-done.21.state, f32[256,4096]{1,0:T(8,128)S(1)} %shard_map.78.intra, ...), custom_call_target="tpu_custom_call", output_to_operand_aliasing={{}: (6, {})} | custom-call | tf_op jit(solution)/shard_map/pallas_call | solution.py:253
  (35 shorter events, 10.7 us)
Async XLA Ops:
  2.8 3.1 %collective-permute-start.1 = (f32[520,512]{1,0:T(8,128)S(1)}, f32[520,512]{1,0:T(8,128)S(1)}, u32[]{:S(2)}, u32[]{:S(2)}) collective-permute-start(f32[520,512]{1,0:T(8,128)S(1)} %get-tuple-element.40.table.refs_6_), channel_id=1, source_target_pairs={{0,1},{1,0},{2,3},{3,2},{4,5},{5,4},{6,7},{7,6},{8,9},{9,8},{10,11... | collective-permute-start | bytes 3194888 | tf_op jit(solution)/shard_map/ppermute | solution.py:285
  4.2 5.9 %collective-permute-start = (f32[512,512]{1,0:T(8,128)S(1)}, f32[512,512]{1,0:T(8,128)S(1)}, u32[]{:S(2)}, u32[]{:S(2)}) collective-permute-start(f32[512,512]{1,0:T(8,128)S(1)} %shard_map.74), channel_id=1, source_target_pairs={{0,1},{1,0},{2,3},{3,2},{4,5},{5,4},{6,7},{7,6},{8,9},{9,8},{10,11... | collective-permute-start | bytes 3145736 | tf_op jit(solution)/shard_map/ppermute | solution.py:285
  6.2 6.0 %collective-permute-start.5 = (bf16[136,512]{1,0:T(8,128)(2,1)S(1)}, bf16[136,512]{1,0:T(8,128)(2,1)S(1)}, u32[]{:S(2)}, u32[]{:S(2)}) collective-permute-start(bf16[136,512]{1,0:T(8,128)(2,1)S(1)} %get-tuple-element.49), channel_id=1, source_target_pairs={{0,2},{2,0},{4,6},{6,4},{1,3},{3,1},{5,7},{7,5},{8,10},{10,8},{12,... | collective-permute-start | bytes 417800 | tf_op jit(solution)/shard_map/ppermute | solution.py:285
  7.5 6.6 %collective-permute-start.6 = (bf16[136,512]{1,0:T(8,128)(2,1)S(1)}, bf16[136,512]{1,0:T(8,128)(2,1)S(1)}, u32[]{:S(2)}, u32[]{:S(2)}) collective-permute-start(bf16[136,512]{1,0:T(8,128)(2,1)S(1)} %get-tuple-element.50), channel_id=1, source_target_pairs={{0,4},{2,6},{4,0},{6,2},{1,5},{3,7},{5,1},{7,3},{8,12},{10,14},{12... | collective-permute-start | bytes 417800 | tf_op jit(solution)/shard_map/ppermute | solution.py:285
  7.6 1.9 %copy-start.1 = (bf16[4096]{0:T(1024)(128)(2,1)S(1)}, bf16[4096]{0:T(1024)(128)(2,1)}, u32[]{:S(2)}) copy-start(bf16[4096]{0:T(1024)(128)(2,1)} %param.13) | copy-start | bytes 24580
  7.6 1.9 %copy-start = (bf16[256,4096]{1,0:T(8,128)(2,1)S(1)}, bf16[256,4096]{1,0:T(8,128)(2,1)}, u32[]{:S(2)}) copy-start(bf16[256,4096]{1,0:T(8,128)(2,1)} %og.1) | copy-start | bytes 6291460
  7.6 13.5 %collective-permute-start.7 = (bf16[136,512]{1,0:T(8,128)(2,1)S(1)}, bf16[136,512]{1,0:T(8,128)(2,1)S(1)}, u32[]{:S(2)}, u32[]{:S(2)}) collective-permute-start(bf16[136,512]{1,0:T(8,128)(2,1)S(1)} %get-tuple-element.51), channel_id=1, source_target_pairs={{0,6},{2,4},{4,2},{6,0},{1,7},{3,5},{5,3},{7,1},{8,14},{10,12},{12... | collective-permute-start | bytes 417800 | tf_op jit(solution)/shard_map/ppermute | solution.py:285
  21.2 5.7 %collective-permute-start.11 = (bf16[136,512]{1,0:T(8,128)(2,1)S(1)}, bf16[136,512]{1,0:T(8,128)(2,1)S(1)}, u32[]{:S(2)}, u32[]{:S(2)}) collective-permute-start(bf16[136,512]{1,0:T(8,128)(2,1)S(1)} %shard_map.81), channel_id=1, source_target_pairs={{0,8},{16,24},{1,9},{17,25},{2,10},{18,26},{3,11},{19,27},{4,12},{... | collective-permute-start | bytes 417800 | tf_op jit(solution)/shard_map/ppermute | solution.py:285
  24.4 5.8 %collective-permute-start.12 = (bf16[136,512]{1,0:T(8,128)(2,1)S(1)}, bf16[136,512]{1,0:T(8,128)(2,1)S(1)}, u32[]{:S(2)}, u32[]{:S(2)}) collective-permute-start(bf16[136,512]{1,0:T(8,128)(2,1)S(1)} %shard_map.81), channel_id=1, source_target_pairs={{0,16},{8,24},{1,17},{9,25},{2,18},{10,26},{3,19},{11,27},{4,20},{... | collective-permute-start | bytes 417800 | tf_op jit(solution)/shard_map/ppermute | solution.py:285
  25.7 6.8 %collective-permute-start.13 = (bf16[136,512]{1,0:T(8,128)(2,1)S(1)}, bf16[136,512]{1,0:T(8,128)(2,1)S(1)}, u32[]{:S(2)}, u32[]{:S(2)}) collective-permute-start(bf16[136,512]{1,0:T(8,128)(2,1)S(1)} %shard_map.81), channel_id=1, source_target_pairs={{0,24},{8,16},{1,25},{9,17},{2,26},{10,18},{3,27},{11,19},{4,28},{... | collective-permute-start | bytes 417800 | tf_op jit(solution)/shard_map/ppermute | solution.py:285
  32.8 3.9 %collective-permute-start.17 = (bf16[128,512]{1,0:T(8,128)(2,1)S(1)}, bf16[128,512]{1,0:T(8,128)(2,1)S(1)}, u32[]{:S(2)}, u32[]{:S(2)}) collective-permute-start(bf16[128,512]{1,0:T(8,128)(2,1)S(1)} %get-tuple-element.57), channel_id=1, source_target_pairs={{0,2},{2,0},{4,6},{6,4},{1,3},{3,1},{5,7},{7,5},{8,10},{10,8},{12,... | collective-permute-start | bytes 393224 | tf_op jit(solution)/shard_map/ppermute | solution.py:285
  32.9 5.1 %collective-permute-start.18 = (bf16[128,512]{1,0:T(8,128)(2,1)S(1)}, bf16[128,512]{1,0:T(8,128)(2,1)S(1)}, u32[]{:S(2)}, u32[]{:S(2)}) collective-permute-start(bf16[128,512]{1,0:T(8,128)(2,1)S(1)} %get-tuple-element.58), channel_id=1, source_target_pairs={{0,4},{2,6},{4,0},{6,2},{1,5},{3,7},{5,1},{7,3},{8,12},{10,14},{12... | collective-permute-start | bytes 393224 | tf_op jit(solution)/shard_map/ppermute | solution.py:285
  34.2 12.2 %collective-permute-start.19 = (bf16[128,512]{1,0:T(8,128)(2,1)S(1)}, bf16[128,512]{1,0:T(8,128)(2,1)S(1)}, u32[]{:S(2)}, u32[]{:S(2)}) collective-permute-start(bf16[128,512]{1,0:T(8,128)(2,1)S(1)} %get-tuple-element.59), channel_id=1, source_target_pairs={{0,6},{2,4},{4,2},{6,0},{1,7},{3,5},{5,3},{7,1},{8,14},{10,12},{12... | collective-permute-start | bytes 393224 | tf_op jit(solution)/shard_map/ppermute | solution.py:285
  46.9 31.9 %collective-permute-start.20 = (bf16[512,512]{1,0:T(8,128)(2,1)S(1)}, bf16[512,512]{1,0:T(8,128)(2,1)S(1)}, u32[]{:S(2)}, u32[]{:S(2)}) collective-permute-start(bf16[512,512]{1,0:T(8,128)(2,1)S(1)} %get-tuple-element.60), channel_id=1, source_target_pairs={{0,1},{1,0},{2,3},{3,2},{4,5},{5,4},{6,7},{7,6},{8,9},{9,8},{10,11... | collective-permute-start | bytes 1572872 | tf_op jit(solution)/shard_map/ppermute | solution.py:285
  49.1 5.0 %collective-permute-start.2 = (bf16[128,512]{1,0:T(8,128)(2,1)S(1)}, bf16[128,512]{1,0:T(8,128)(2,1)S(1)}, u32[]{:S(2)}, u32[]{:S(2)}) collective-permute-start(bf16[128,512]{1,0:T(8,128)(2,1)S(1)} %get-tuple-element.42), channel_id=1, source_target_pairs={{0,2},{2,0},{4,6},{6,4},{1,3},{3,1},{5,7},{7,5},{8,10},{10,8},{12,... | collective-permute-start | bytes 393224 | tf_op jit(solution)/shard_map/ppermute | solution.py:285
  49.1 7.6 %collective-permute-start.3 = (bf16[128,512]{1,0:T(8,128)(2,1)S(1)}, bf16[128,512]{1,0:T(8,128)(2,1)S(1)}, u32[]{:S(2)}, u32[]{:S(2)}) collective-permute-start(bf16[128,512]{1,0:T(8,128)(2,1)S(1)} %get-tuple-element.43), channel_id=1, source_target_pairs={{0,4},{2,6},{4,0},{6,2},{1,5},{3,7},{5,1},{7,3},{8,12},{10,14},{12... | collective-permute-start | bytes 393224 | tf_op jit(solution)/shard_map/ppermute | solution.py:285
  50.3 13.0 %collective-permute-start.4 = (bf16[128,512]{1,0:T(8,128)(2,1)S(1)}, bf16[128,512]{1,0:T(8,128)(2,1)S(1)}, u32[]{:S(2)}, u32[]{:S(2)}) collective-permute-start(bf16[128,512]{1,0:T(8,128)(2,1)S(1)} %get-tuple-element.44), channel_id=1, source_target_pairs={{0,6},{2,4},{4,2},{6,0},{1,7},{3,5},{5,3},{7,1},{8,14},{10,12},{12... | collective-permute-start | bytes 393224 | tf_op jit(solution)/shard_map/ppermute | solution.py:285
  63.5 4.8 %collective-permute-start.8 = (bf16[128,512]{1,0:T(8,128)(2,1)S(1)}, bf16[128,512]{1,0:T(8,128)(2,1)S(1)}, u32[]{:S(2)}, u32[]{:S(2)}) collective-permute-start(bf16[128,512]{1,0:T(8,128)(2,1)S(1)} %shard_map.80), channel_id=1, source_target_pairs={{0,8},{16,24},{1,9},{17,25},{2,10},{18,26},{3,11},{19,27},{4,12},{... | collective-permute-start | bytes 393224 | tf_op jit(solution)/shard_map/ppermute | solution.py:285
  65.7 5.7 %collective-permute-start.9 = (bf16[128,512]{1,0:T(8,128)(2,1)S(1)}, bf16[128,512]{1,0:T(8,128)(2,1)S(1)}, u32[]{:S(2)}, u32[]{:S(2)}) collective-permute-start(bf16[128,512]{1,0:T(8,128)(2,1)S(1)} %shard_map.80), channel_id=1, source_target_pairs={{0,16},{8,24},{1,17},{9,25},{2,18},{10,26},{3,19},{11,27},{4,20},{... | collective-permute-start | bytes 393224 | tf_op jit(solution)/shard_map/ppermute | solution.py:285
  67.0 6.7 %collective-permute-start.10 = (bf16[128,512]{1,0:T(8,128)(2,1)S(1)}, bf16[128,512]{1,0:T(8,128)(2,1)S(1)}, u32[]{:S(2)}, u32[]{:S(2)}) collective-permute-start(bf16[128,512]{1,0:T(8,128)(2,1)S(1)} %shard_map.80), channel_id=1, source_target_pairs={{0,24},{8,16},{1,25},{9,17},{2,26},{10,18},{3,27},{11,19},{4,28},{... | collective-permute-start | bytes 393224 | tf_op jit(solution)/shard_map/ppermute | solution.py:285
  74.1 6.6 %collective-permute-start.14 = (bf16[128,512]{1,0:T(8,128)(2,1)S(1)}, bf16[128,512]{1,0:T(8,128)(2,1)S(1)}, u32[]{:S(2)}, u32[]{:S(2)}) collective-permute-start(bf16[128,512]{1,0:T(8,128)(2,1)S(1)} %get-tuple-element.53), channel_id=1, source_target_pairs={{0,2},{2,0},{4,6},{6,4},{1,3},{3,1},{5,7},{7,5},{8,10},{10,8},{12,... | collective-permute-start | bytes 393224 | tf_op jit(solution)/shard_map/ppermute | solution.py:285
  74.2 6.5 %collective-permute-start.15 = (bf16[128,512]{1,0:T(8,128)(2,1)S(1)}, bf16[128,512]{1,0:T(8,128)(2,1)S(1)}, u32[]{:S(2)}, u32[]{:S(2)}) collective-permute-start(bf16[128,512]{1,0:T(8,128)(2,1)S(1)} %get-tuple-element.54), channel_id=1, source_target_pairs={{0,4},{2,6},{4,0},{6,2},{1,5},{3,7},{5,1},{7,3},{8,12},{10,14},{12... | collective-permute-start | bytes 393224 | tf_op jit(solution)/shard_map/ppermute | solution.py:285
  75.5 12.8 %collective-permute-start.16 = (bf16[128,512]{1,0:T(8,128)(2,1)S(1)}, bf16[128,512]{1,0:T(8,128)(2,1)S(1)}, u32[]{:S(2)}, u32[]{:S(2)}) collective-permute-start(bf16[128,512]{1,0:T(8,128)(2,1)S(1)} %get-tuple-element.55), channel_id=1, source_target_pairs={{0,6},{2,4},{4,2},{6,0},{1,7},{3,5},{5,3},{7,1},{8,14},{10,12},{12... | collective-permute-start | bytes 393224 | tf_op jit(solution)/shard_map/ppermute | solution.py:285
  88.8 3.5 %collective-permute-start.21 = (bf16[512,512]{1,0:T(8,128)(2,1)S(1)}, bf16[512,512]{1,0:T(8,128)(2,1)S(1)}, u32[]{:S(2)}, u32[]{:S(2)}) collective-permute-start(bf16[512,512]{1,0:T(8,128)(2,1)S(1)} %get-tuple-element.63), channel_id=1, source_target_pairs={{0,1},{1,0},{2,3},{3,2},{4,5},{5,4},{6,7},{7,6},{8,9},{9,8},{10,11... | collective-permute-start | bytes 1572872 | tf_op jit(solution)/shard_map/ppermute | solution.py:285
where the time goes:
time: 94.6 us; the launch traced here: 94.2 us
  waiting for transfers between devices  51 us (54%)
  starting transfers between devices  25.8 us (27%)
  Pallas kernels  17.2 us (18%)
    ppermute x22, waiting for transfers between devices, swap(): return lax.ppermute(a, axis, pairs)  51 us
    ppermute x22, starting transfers between devices, swap(): return lax.ppermute(a, axis, pairs)  25.8 us
    pallas_call x4, Pallas kernels, final(): pl.pallas_call(functools.partial(final_kernel, first=first, per=per, half...  7.7 us
    pallas_call x13, Pallas kernels, call(): pl.pallas_call(kernel, out_shape=outs, in_specs=[vmem] * len(ins), out_sp...  6.66 us
    pallas_call x1, Pallas kernels, shards(): pl.pallas_call(functools.partial(first_kernel, scale=scale, first=half, p...  2.84 us
  transfers between devices with their start and end apart: 22, of which 14 were waited for; matrix products, arithmetic and copies ran while one was open for 0% of the time, Pallas kernels for 12%

commit v1 on v0

--- a/solution.py
+++ b/solution.py
@@ -280,8 +280,8 @@
     assert nz & (nz - 1) == 0 and spans & (spans - 1) == 0
     scale = math.sqrt(dkey)
 
-    def swap(a, axis, bit, up=False):
-        pairs = [(j, j ^ bit) for j in range(lax.axis_size(axis)) if not up or j < j ^ bit]
+    def swap(a, axis, bit):
+        pairs = [(j, j ^ bit) for j in range(lax.axis_size(axis))]
         return lax.ppermute(a, axis, pairs)
 
     vmem, hbm = pl.BlockSpec(memory_space=pltpu.VMEM), pl.BlockSpec(memory_space=pltpu.HBM)
@@ -346,7 +346,7 @@
             [shape((rows + pads[i], dval), BF16)],
             sent[i] + (sent[0] if i else []),
         )[0]
-        cumuls.append([swap(total, "seq", k, up=True) for k in range(1, spans)])
+        cumuls.append([swap(total, "seq", k) for k in range(1, spans)])
         pres = call(
             functools.partial(prefix_kernel, rows=rows, nz=nz, spans=spans, chunk=i),
             [shape((rows, dval), BF16)] * nz,

time: 94.6 us -> 88.4 us (0.934)
  the two profiles are of different devices: /device:TPU:21 before, /device:TPU:1 now
where the time goes in v1:
time: 88.4 us; the launch traced here: 88.1 us
  starting transfers between devices  36.8 us (42%)
  waiting for transfers between devices  33 us (37%)
  Pallas kernels  17.2 us (19%)
  local copies, waits for them, and re-layouts  1.02 us (1%)
    ppermute x22, starting transfers between devices, swap(): return lax.ppermute(a, axis, pairs)  36.8 us
    ppermute x22, waiting for transfers between devices, swap(): return lax.ppermute(a, axis, pairs)  33 us
    pallas_call x4, Pallas kernels, final(): pl.pallas_call(functools.partial(final_kernel, first=first, per=per, half...  7.7 us
    pallas_call x13, Pallas kernels, call(): pl.pallas_call(kernel, out_shape=outs, in_specs=[vmem] * len(ins), out_sp...  6.65 us
    pallas_call x1, Pallas kernels, shards(): pl.pallas_call(functools.partial(first_kernel, scale=scale, first=half, p...  2.84 us
  transfers between devices with their start and end apart: 22, of which 15 were waited for; matrix products, arithmetic and copies ran while one was open for 0% of the time, Pallas kernels for 12%

profile of v1, /device:TPU:1, one launch (start us, length us, event | category | flops | bytes accessed | tf_op | source)
XLA Modules:
  0.0 88.1 jit_solution(1567038666769644192)
XLA Ops:
  0.0 2.8 %first.1 = (f32[8,256]{1,0:T(8,128)S(1)}, f32[256,24]{1,0:T(8,128)S(1)}, f32[520,512]{1,0:T(8,128)S(1)}, s32[1]{0:T(128)}, bf16[256,2048]{1,0:T(8,128)(2,1)S(1)}...) custom-call(bf16[8,256]{1,0:T(8,128)(2,1)} %bitcast.2, bf16[8,256]{1,0:T(8,128)(2,1)} %bitcast.3, ...), custom_call_target="tpu_custom_call" | custom-call | tf_op jit(solution)/shard_map/first/pallas_call | solution.py:289
  5.9 2.5 %collective-permute-start.5 = (bf16[136,512]{1,0:T(8,128)(2,1)S(1)}, bf16[136,512]{1,0:T(8,128)(2,1)S(1)}, u32[]{:S(2)}, u32[]{:S(2)}) collective-permute-start(bf16[136,512]{1,0:T(8,128)(2,1)S(1)} %get-tuple-element.49), channel_id=1, source_target_pairs={{0,2},{2,0},{4,6},{6,4},{1,3},{3,1},{5,7},{7,5},{8,10},{10,8},{12,... | collective-permute-start | bytes 417800 | tf_op jit(solution)/shard_map/ppermute | solution.py:285
  8.3 2.3 %collective-permute-start.6 = (bf16[136,512]{1,0:T(8,128)(2,1)S(1)}, bf16[136,512]{1,0:T(8,128)(2,1)S(1)}, u32[]{:S(2)}, u32[]{:S(2)}) collective-permute-start(bf16[136,512]{1,0:T(8,128)(2,1)S(1)} %get-tuple-element.50), channel_id=1, source_target_pairs={{0,4},{2,6},{4,0},{6,2},{1,5},{3,7},{5,1},{7,3},{8,12},{10,14},{12... | collective-permute-start | bytes 417800 | tf_op jit(solution)/shard_map/ppermute | solution.py:285
  13.0 1.8 %shard_map.78.intra = f32[256,4096]{1,0:T(8,128)S(1)} custom-call(bf16[256,2048]{1,0:T(8,128)(2,1)S(1)} %get-tuple-element.36.q, bf16[256,2048]{1,0:T(8,128)(2,1)S(1)} %get-tuple-element.37.k, bf16[256,4096]{1,0:T(8,128)(2,1)S(1)} %get-tuple-element.38.v, f32[8,256]{1,0:T(8,128)S(1)} %get-tuple-element.46.rowa, f32[256,24]{1,0:T(8,128)S(1)} %get-tuple-element.47.cols), custom_call_target="tpu_custom_call" | custom-call | tf_op jit(solution)/shard_map/pallas_call | solution.py:23
  14.9 5.1 %collective-permute-done.7.refs_7_.refs_3_.refs_10_ = bf16[136,512]{1,0:T(8,128)(2,1)S(1)} collective-permute-done((bf16[136,512]{1,0:T(8,128)(2,1)S(1)}, bf16[136,512]{1,0:T(8,128)(2,1)S(1)}, u32[]{:S(2)}, u32[]{:S(2)}) %collective-permute-start.7) | collective-permute-done | bytes 139296 | tf_op jit(solution)/shard_map/ppermute | solution.py:285
  20.1 1.3 %collective-permute-start.11 = (bf16[136,512]{1,0:T(8,128)(2,1)S(1)}, bf16[136,512]{1,0:T(8,128)(2,1)S(1)}, u32[]{:S(2)}, u32[]{:S(2)}) collective-permute-start(bf16[136,512]{1,0:T(8,128)(2,1)S(1)} %shard_map.81), channel_id=1, source_target_pairs={{0,8},{8,0},{16,24},{24,16},{1,9},{9,1},{17,25},{25,17},{2,10},{10... | collective-permute-start | bytes 417800 | tf_op jit(solution)/shard_map/ppermute | solution.py:285
  21.4 1.2 %collective-permute-start.12 = (bf16[136,512]{1,0:T(8,128)(2,1)S(1)}, bf16[136,512]{1,0:T(8,128)(2,1)S(1)}, u32[]{:S(2)}, u32[]{:S(2)}) collective-permute-start(bf16[136,512]{1,0:T(8,128)(2,1)S(1)} %shard_map.81), channel_id=1, source_target_pairs={{0,16},{8,24},{16,0},{24,8},{1,17},{9,25},{17,1},{25,9},{2,18},{10... | collective-permute-start | bytes 417800 | tf_op jit(solution)/shard_map/ppermute | solution.py:285
  22.8 1.3 %collective-permute-done.11.refs_11_.refs_4_ = bf16[136,512]{1,0:T(8,128)(2,1)S(1)} collective-permute-done((bf16[136,512]{1,0:T(8,128)(2,1)S(1)}, bf16[136,512]{1,0:T(8,128)(2,1)S(1)}, u32[]{:S(2)}, u32[]{:S(2)}) %collective-permute-start.11) | collective-permute-done | bytes 139296 | tf_op jit(solution)/shard_map/ppermute | solution.py:285
  24.1 1.3 %collective-permute-done.12.refs_12_.refs_5_ = bf16[136,512]{1,0:T(8,128)(2,1)S(1)} collective-permute-done((bf16[136,512]{1,0:T(8,128)(2,1)S(1)}, bf16[136,512]{1,0:T(8,128)(2,1)S(1)}, u32[]{:S(2)}, u32[]{:S(2)}) %collective-permute-start.12) | collective-permute-done | bytes 139296 | tf_op jit(solution)/shard_map/ppermute | solution.py:285
  25.4 3.0 %collective-permute-done.13.refs_13_.refs_6_ = bf16[136,512]{1,0:T(8,128)(2,1)S(1)} collective-permute-done((bf16[136,512]{1,0:T(8,128)(2,1)S(1)}, bf16[136,512]{1,0:T(8,128)(2,1)S(1)}, u32[]{:S(2)}, u32[]{:S(2)}) %collective-permute-start.13) | collective-permute-done | bytes 139296 | tf_op jit(solution)/shard_map/ppermute | solution.py:285
  28.7 3.7 %collective-permute-start.17 = (bf16[128,512]{1,0:T(8,128)(2,1)S(1)}, bf16[128,512]{1,0:T(8,128)(2,1)S(1)}, u32[]{:S(2)}, u32[]{:S(2)}) collective-permute-start(bf16[128,512]{1,0:T(8,128)(2,1)S(1)} %get-tuple-element.57), channel_id=1, source_target_pairs={{0,2},{2,0},{4,6},{6,4},{1,3},{3,1},{5,7},{7,5},{8,10},{10,8},{12,... | collective-permute-start | bytes 393224 | tf_op jit(solution)/shard_map/ppermute | solution.py:285
  32.4 1.1 %collective-permute-start.18 = (bf16[128,512]{1,0:T(8,128)(2,1)S(1)}, bf16[128,512]{1,0:T(8,128)(2,1)S(1)}, u32[]{:S(2)}, u32[]{:S(2)}) collective-permute-start(bf16[128,512]{1,0:T(8,128)(2,1)S(1)} %get-tuple-element.58), channel_id=1, source_target_pairs={{0,4},{2,6},{4,0},{6,2},{1,5},{3,7},{5,1},{7,3},{8,12},{10,14},{12... | collective-permute-start | bytes 393224 | tf_op jit(solution)/shard_map/ppermute | solution.py:285
  33.5 1.1 %collective-permute-start.19 = (bf16[128,512]{1,0:T(8,128)(2,1)S(1)}, bf16[128,512]{1,0:T(8,128)(2,1)S(1)}, u32[]{:S(2)}, u32[]{:S(2)}) collective-permute-start(bf16[128,512]{1,0:T(8,128)(2,1)S(1)} %get-tuple-element.59), channel_id=1, source_target_pairs={{0,6},{2,4},{4,2},{6,0},{1,7},{3,5},{5,3},{7,1},{8,14},{10,12},{12... | collective-permute-start | bytes 393224 | tf_op jit(solution)/shard_map/ppermute | solution.py:285
  34.8 3.9 %collective-permute-done.18.refs_2_ = bf16[128,512]{1,0:T(8,128)(2,1)S(1)} collective-permute-done((bf16[128,512]{1,0:T(8,128)(2,1)S(1)}, bf16[128,512]{1,0:T(8,128)(2,1)S(1)}, u32[]{:S(2)}, u32[]{:S(2)}) %collective-permute-start.18) | collective-permute-done | bytes 131104 | tf_op jit(solution)/shard_map/ppermute | solution.py:285
  38.6 2.6 %collective-permute-done.19.refs_3_ = bf16[128,512]{1,0:T(8,128)(2,1)S(1)} collective-permute-done((bf16[128,512]{1,0:T(8,128)(2,1)S(1)}, bf16[128,512]{1,0:T(8,128)(2,1)S(1)}, u32[]{:S(2)}, u32[]{:S(2)}) %collective-permute-start.19) | collective-permute-done | bytes 131104 | tf_op jit(solution)/shard_map/ppermute | solution.py:285
  41.7 5.1 %collective-permute-start.20 = (bf16[512,512]{1,0:T(8,128)(2,1)S(1)}, bf16[512,512]{1,0:T(8,128)(2,1)S(1)}, u32[]{:S(2)}, u32[]{:S(2)}) collective-permute-start(bf16[512,512]{1,0:T(8,128)(2,1)S(1)} %get-tuple-element.60), channel_id=1, source_target_pairs={{0,1},{1,0},{2,3},{3,2},{4,5},{5,4},{6,7},{7,6},{8,9},{9,8},{10,11... | collective-permute-start | bytes 1572872 | tf_op jit(solution)/shard_map/ppermute | solution.py:285
  46.8 1.7 %collective-permute-start.2 = (bf16[128,512]{1,0:T(8,128)(2,1)S(1)}, bf16[128,512]{1,0:T(8,128)(2,1)S(1)}, u32[]{:S(2)}, u32[]{:S(2)}) collective-permute-start(bf16[128,512]{1,0:T(8,128)(2,1)S(1)} %get-tuple-element.42), channel_id=1, source_target_pairs={{0,2},{2,0},{4,6},{6,4},{1,3},{3,1},{5,7},{7,5},{8,10},{10,8},{12,... | collective-permute-start | bytes 393224 | tf_op jit(solution)/shard_map/ppermute | solution.py:285
  49.5 1.2 %collective-permute-start.4 = (bf16[128,512]{1,0:T(8,128)(2,1)S(1)}, bf16[128,512]{1,0:T(8,128)(2,1)S(1)}, u32[]{:S(2)}, u32[]{:S(2)}) collective-permute-start(bf16[128,512]{1,0:T(8,128)(2,1)S(1)} %get-tuple-element.44), channel_id=1, source_target_pairs={{0,6},{2,4},{4,2},{6,0},{1,7},{3,5},{5,3},{7,1},{8,14},{10,12},{12... | collective-permute-start | bytes 393224 | tf_op jit(solution)/shard_map/ppermute | solution.py:285
  50.7 3.6 %collective-permute-done.2.refs_1_ = bf16[128,512]{1,0:T(8,128)(2,1)S(1)} collective-permute-done((bf16[128,512]{1,0:T(8,128)(2,1)S(1)}, bf16[128,512]{1,0:T(8,128)(2,1)S(1)}, u32[]{:S(2)}, u32[]{:S(2)}) %collective-permute-start.2) | collective-permute-done | bytes 131104 | tf_op jit(solution)/shard_map/ppermute | solution.py:285
  54.3 5.6 %collective-permute-done.4.refs_3_ = bf16[128,512]{1,0:T(8,128)(2,1)S(1)} collective-permute-done((bf16[128,512]{1,0:T(8,128)(2,1)S(1)}, bf16[128,512]{1,0:T(8,128)(2,1)S(1)}, u32[]{:S(2)}, u32[]{:S(2)}) %collective-permute-start.4) | collective-permute-done | bytes 131104 | tf_op jit(solution)/shard_map/ppermute | solution.py:285
  60.5 2.3 %collective-permute-start.10 = (bf16[128,512]{1,0:T(8,128)(2,1)S(1)}, bf16[128,512]{1,0:T(8,128)(2,1)S(1)}, u32[]{:S(2)}, u32[]{:S(2)}) collective-permute-start(bf16[128,512]{1,0:T(8,128)(2,1)S(1)} %shard_map.80), channel_id=1, source_target_pairs={{0,24},{8,16},{16,8},{24,0},{1,25},{9,17},{17,9},{25,1},{2,26},{10... | collective-permute-start | bytes 393224 | tf_op jit(solution)/shard_map/ppermute | solution.py:285
  62.7 1.2 %collective-permute-done.8.refs_4_ = bf16[128,512]{1,0:T(8,128)(2,1)S(1)} collective-permute-done((bf16[128,512]{1,0:T(8,128)(2,1)S(1)}, bf16[128,512]{1,0:T(8,128)(2,1)S(1)}, u32[]{:S(2)}, u32[]{:S(2)}) %collective-permute-start.8) | collective-permute-done | bytes 131104 | tf_op jit(solution)/shard_map/ppermute | solution.py:285
  63.9 1.6 %collective-permute-done.9.refs_5_ = bf16[128,512]{1,0:T(8,128)(2,1)S(1)} collective-permute-done((bf16[128,512]{1,0:T(8,128)(2,1)S(1)}, bf16[128,512]{1,0:T(8,128)(2,1)S(1)}, u32[]{:S(2)}, u32[]{:S(2)}) %collective-permute-start.9) | collective-permute-done | bytes 131104 | tf_op jit(solution)/shard_map/ppermute | solution.py:285
  66.2 3.6 %collective-permute-start.14 = (bf16[128,512]{1,0:T(8,128)(2,1)S(1)}, bf16[128,512]{1,0:T(8,128)(2,1)S(1)}, u32[]{:S(2)}, u32[]{:S(2)}) collective-permute-start(bf16[128,512]{1,0:T(8,128)(2,1)S(1)} %get-tuple-element.53), channel_id=1, source_target_pairs={{0,2},{2,0},{4,6},{6,4},{1,3},{3,1},{5,7},{7,5},{8,10},{10,8},{12,... | collective-permute-start | bytes 393224 | tf_op jit(solution)/shard_map/ppermute | solution.py:285
  69.8 1.1 %collective-permute-start.15 = (bf16[128,512]{1,0:T(8,128)(2,1)S(1)}, bf16[128,512]{1,0:T(8,128)(2,1)S(1)}, u32[]{:S(2)}, u32[]{:S(2)}) collective-permute-start(bf16[128,512]{1,0:T(8,128)(2,1)S(1)} %get-tuple-element.54), channel_id=1, source_target_pairs={{0,4},{2,6},{4,0},{6,2},{1,5},{3,7},{5,1},{7,3},{8,12},{10,14},{12... | collective-permute-start | bytes 393224 | tf_op jit(solution)/shard_map/ppermute | solution.py:285
  70.9 1.1 %collective-permute-start.16 = (bf16[128,512]{1,0:T(8,128)(2,1)S(1)}, bf16[128,512]{1,0:T(8,128)(2,1)S(1)}, u32[]{:S(2)}, u32[]{:S(2)}) collective-permute-start(bf16[128,512]{1,0:T(8,128)(2,1)S(1)} %get-tuple-element.55), channel_id=1, source_target_pairs={{0,6},{2,4},{4,2},{6,0},{1,7},{3,5},{5,3},{7,1},{8,14},{10,12},{12... | collective-permute-start | bytes 393224 | tf_op jit(solution)/shard_map/ppermute | solution.py:285
  72.0 1.9 %shard_map.85.rest_0_ = bf16[256,4096]{1,0:T(8,128)(2,1)} custom-call(s32[1]{0:T(128)} %get-tuple-element.35.core, bf16[256,2048]{1,0:T(8,128)(2,1)S(1)} %get-tuple-element.36.q, bf16[512,512]{1,0:T(8,128)(2,1)S(1)} %get-tuple-element.61.state, f32[256,4096]{1,0:T(8,128)S(1)} %shard_map.78.intra, f32[256,24]{1,0:T(8,128)S(1)} %get-tuple-element.47.cols, ...), custom_call_target="tpu_custom_call" | custom-call | tf_op jit(solution)/shard_map/pallas_call | solution.py:253
  73.9 1.9 %shard_map.86.rest_0_ = bf16[256,4096]{1,0:T(8,128)(2,1)} custom-call(s32[1]{0:T(128)} %get-tuple-element.35.core, bf16[256,2048]{1,0:T(8,128)(2,1)S(1)} %get-tuple-element.36.q, bf16[512,512]{1,0:T(8,128)(2,1)S(1)} %collective-permute-done.20.state, f32[256,4096]{1,0:T(8,128)S(1)} %shard_map.78.intra, ...), custom_call_target="tpu_custom_call", output_to_operand_aliasing={{}: (6, {})} | custom-call | tf_op jit(solution)/shard_map/pallas_call | solution.py:253
  76.3 2.2 %collective-permute-done.16.refs_3_ = bf16[128,512]{1,0:T(8,128)(2,1)S(1)} collective-permute-done((bf16[128,512]{1,0:T(8,128)(2,1)S(1)}, bf16[128,512]{1,0:T(8,128)(2,1)S(1)}, u32[]{:S(2)}, u32[]{:S(2)}) %collective-permute-start.16) | collective-permute-done | bytes 131104 | tf_op jit(solution)/shard_map/ppermute | solution.py:285
  79.0 5.3 %collective-permute-start.21 = (bf16[512,512]{1,0:T(8,128)(2,1)S(1)}, bf16[512,512]{1,0:T(8,128)(2,1)S(1)}, u32[]{:S(2)}, u32[]{:S(2)}) collective-permute-start(bf16[512,512]{1,0:T(8,128)(2,1)S(1)} %get-tuple-element.63), channel_id=1, source_target_pairs={{0,1},{1,0},{2,3},{3,2},{4,5},{5,4},{6,7},{7,6},{8,9},{9,8},{10,11... | collective-permute-start | bytes 1572872 | tf_op jit(solution)/shard_map/ppermute | solution.py:285
  84.3 1.9 %shard_map.88.rest_0_ = bf16[256,4096]{1,0:T(8,128)(2,1)} custom-call(s32[1]{0:T(128)} %get-tuple-element.35.core, bf16[256,2048]{1,0:T(8,128)(2,1)S(1)} %get-tuple-element.36.q, bf16[512,512]{1,0:T(8,128)(2,1)S(1)} %get-tuple-element.64.state, f32[256,4096]{1,0:T(8,128)S(1)} %shard_map.78.intra, ...), custom_call_target="tpu_custom_call", output_to_operand_aliasing={{}: (6, {})} | custom-call | tf_op jit(solution)/shard_map/pallas_call | solution.py:253
  86.2 1.9 %shard_map.89 = bf16[256,4096]{1,0:T(8,128)(2,1)} custom-call(s32[1]{0:T(128)} %get-tuple-element.35.core, bf16[256,2048]{1,0:T(8,128)(2,1)S(1)} %get-tuple-element.36.q, bf16[512,512]{1,0:T(8,128)(2,1)S(1)} %collective-permute-done.21.state, f32[256,4096]{1,0:T(8,128)S(1)} %shard_map.78.intra, ...), custom_call_target="tpu_custom_call", output_to_operand_aliasing={{}: (6, {})} | custom-call | tf_op jit(solution)/shard_map/pallas_call | solution.py:253
  (35 shorter events, 10.0 us)
Async XLA Ops:
  2.8 2.7 %collective-permute-start.1 = (f32[520,512]{1,0:T(8,128)S(1)}, f32[520,512]{1,0:T(8,128)S(1)}, u32[]{:S(2)}, u32[]{:S(2)}) collective-permute-start(f32[520,512]{1,0:T(8,128)S(1)} %get-tuple-element.40.table.refs_6_), channel_id=1, source_target_pairs={{0,1},{1,0},{2,3},{3,2},{4,5},{5,4},{6,7},{7,6},{8,9},{9,8},{10,11... | collective-permute-start | bytes 3194888 | tf_op jit(solution)/shard_map/ppermute | solution.py:285
  3.5 9.3 %collective-permute-start = (f32[512,512]{1,0:T(8,128)S(1)}, f32[512,512]{1,0:T(8,128)S(1)}, u32[]{:S(2)}, u32[]{:S(2)}) collective-permute-start(f32[512,512]{1,0:T(8,128)S(1)} %shard_map.74), channel_id=1, source_target_pairs={{0,1},{1,0},{2,3},{3,2},{4,5},{5,4},{6,7},{7,6},{8,9},{9,8},{10,11... | collective-permute-start | bytes 3145736 | tf_op jit(solution)/shard_map/ppermute | solution.py:285
  5.9 9.0 %collective-permute-start.5 = (bf16[136,512]{1,0:T(8,128)(2,1)S(1)}, bf16[136,512]{1,0:T(8,128)(2,1)S(1)}, u32[]{:S(2)}, u32[]{:S(2)}) collective-permute-start(bf16[136,512]{1,0:T(8,128)(2,1)S(1)} %get-tuple-element.49), channel_id=1, source_target_pairs={{0,2},{2,0},{4,6},{6,4},{1,3},{3,1},{5,7},{7,5},{8,10},{10,8},{12,... | collective-permute-start | bytes 417800 | tf_op jit(solution)/shard_map/ppermute | solution.py:285
  8.3 6.5 %collective-permute-start.6 = (bf16[136,512]{1,0:T(8,128)(2,1)S(1)}, bf16[136,512]{1,0:T(8,128)(2,1)S(1)}, u32[]{:S(2)}, u32[]{:S(2)}) collective-permute-start(bf16[136,512]{1,0:T(8,128)(2,1)S(1)} %get-tuple-element.50), channel_id=1, source_target_pairs={{0,4},{2,6},{4,0},{6,2},{1,5},{3,7},{5,1},{7,3},{8,12},{10,14},{12... | collective-permute-start | bytes 417800 | tf_op jit(solution)/shard_map/ppermute | solution.py:285
  10.6 0.7 copy-start.1
  10.6 1.6 %copy-start = (bf16[256,4096]{1,0:T(8,128)(2,1)S(1)}, bf16[256,4096]{1,0:T(8,128)(2,1)}, u32[]{:S(2)}) copy-start(bf16[256,4096]{1,0:T(8,128)(2,1)} %og.1) | copy-start | bytes 6291460
  10.7 9.3 %collective-permute-start.7 = (bf16[136,512]{1,0:T(8,128)(2,1)S(1)}, bf16[136,512]{1,0:T(8,128)(2,1)S(1)}, u32[]{:S(2)}, u32[]{:S(2)}) collective-permute-start(bf16[136,512]{1,0:T(8,128)(2,1)S(1)} %get-tuple-element.51), channel_id=1, source_target_pairs={{0,6},{2,4},{4,2},{6,0},{1,7},{3,5},{5,3},{7,1},{8,14},{10,12},{12... | collective-permute-start | bytes 417800 | tf_op jit(solution)/shard_map/ppermute | solution.py:285
  20.1 4.0 %collective-permute-start.11 = (bf16[136,512]{1,0:T(8,128)(2,1)S(1)}, bf16[136,512]{1,0:T(8,128)(2,1)S(1)}, u32[]{:S(2)}, u32[]{:S(2)}) collective-permute-start(bf16[136,512]{1,0:T(8,128)(2,1)S(1)} %shard_map.81), channel_id=1, source_target_pairs={{0,8},{8,0},{16,24},{24,16},{1,9},{9,1},{17,25},{25,17},{2,10},{10... | collective-permute-start | bytes 417800 | tf_op jit(solution)/shard_map/ppermute | solution.py:285
  21.4 4.0 %collective-permute-start.12 = (bf16[136,512]{1,0:T(8,128)(2,1)S(1)}, bf16[136,512]{1,0:T(8,128)(2,1)S(1)}, u32[]{:S(2)}, u32[]{:S(2)}) collective-permute-start(bf16[136,512]{1,0:T(8,128)(2,1)S(1)} %shard_map.81), channel_id=1, source_target_pairs={{0,16},{8,24},{16,0},{24,8},{1,17},{9,25},{17,1},{25,9},{2,18},{10... | collective-permute-start | bytes 417800 | tf_op jit(solution)/shard_map/ppermute | solution.py:285
  22.6 5.8 %collective-permute-start.13 = (bf16[136,512]{1,0:T(8,128)(2,1)S(1)}, bf16[136,512]{1,0:T(8,128)(2,1)S(1)}, u32[]{:S(2)}, u32[]{:S(2)}) collective-permute-start(bf16[136,512]{1,0:T(8,128)(2,1)S(1)} %shard_map.81), channel_id=1, source_target_pairs={{0,24},{8,16},{16,8},{24,0},{1,25},{9,17},{17,9},{25,1},{2,26},{10... | collective-permute-start | bytes 417800 | tf_op jit(solution)/shard_map/ppermute | solution.py:285
  28.7 6.0 %collective-permute-start.17 = (bf16[128,512]{1,0:T(8,128)(2,1)S(1)}, bf16[128,512]{1,0:T(8,128)(2,1)S(1)}, u32[]{:S(2)}, u32[]{:S(2)}) collective-permute-start(bf16[128,512]{1,0:T(8,128)(2,1)S(1)} %get-tuple-element.57), channel_id=1, source_target_pairs={{0,2},{2,0},{4,6},{6,4},{1,3},{3,1},{5,7},{7,5},{8,10},{10,8},{12,... | collective-permute-start | bytes 393224 | tf_op jit(solution)/shard_map/ppermute | solution.py:285
  32.4 6.2 %collective-permute-start.18 = (bf16[128,512]{1,0:T(8,128)(2,1)S(1)}, bf16[128,512]{1,0:T(8,128)(2,1)S(1)}, u32[]{:S(2)}, u32[]{:S(2)}) collective-permute-start(bf16[128,512]{1,0:T(8,128)(2,1)S(1)} %get-tuple-element.58), channel_id=1, source_target_pairs={{0,4},{2,6},{4,0},{6,2},{1,5},{3,7},{5,1},{7,3},{8,12},{10,14},{12... | collective-permute-start | bytes 393224 | tf_op jit(solution)/shard_map/ppermute | solution.py:285
  33.5 7.7 %collective-permute-start.19 = (bf16[128,512]{1,0:T(8,128)(2,1)S(1)}, bf16[128,512]{1,0:T(8,128)(2,1)S(1)}, u32[]{:S(2)}, u32[]{:S(2)}) collective-permute-start(bf16[128,512]{1,0:T(8,128)(2,1)S(1)} %get-tuple-element.59), channel_id=1, source_target_pairs={{0,6},{2,4},{4,2},{6,0},{1,7},{3,5},{5,3},{7,1},{8,14},{10,12},{12... | collective-permute-start | bytes 393224 | tf_op jit(solution)/shard_map/ppermute | solution.py:285
  41.7 32.2 %collective-permute-start.20 = (bf16[512,512]{1,0:T(8,128)(2,1)S(1)}, bf16[512,512]{1,0:T(8,128)(2,1)S(1)}, u32[]{:S(2)}, u32[]{:S(2)}) collective-permute-start(bf16[512,512]{1,0:T(8,128)(2,1)S(1)} %get-tuple-element.60), channel_id=1, source_target_pairs={{0,1},{1,0},{2,3},{3,2},{4,5},{5,4},{6,7},{7,6},{8,9},{9,8},{10,11... | collective-permute-start | bytes 1572872 | tf_op jit(solution)/shard_map/ppermute | solution.py:285
  46.8 7.5 %collective-permute-start.2 = (bf16[128,512]{1,0:T(8,128)(2,1)S(1)}, bf16[128,512]{1,0:T(8,128)(2,1)S(1)}, u32[]{:S(2)}, u32[]{:S(2)}) collective-permute-start(bf16[128,512]{1,0:T(8,128)(2,1)S(1)} %get-tuple-element.42), channel_id=1, source_target_pairs={{0,2},{2,0},{4,6},{6,4},{1,3},{3,1},{5,7},{7,5},{8,10},{10,8},{12,... | collective-permute-start | bytes 393224 | tf_op jit(solution)/shard_map/ppermute | solution.py:285
  48.5 5.8 %collective-permute-start.3 = (bf16[128,512]{1,0:T(8,128)(2,1)S(1)}, bf16[128,512]{1,0:T(8,128)(2,1)S(1)}, u32[]{:S(2)}, u32[]{:S(2)}) collective-permute-start(bf16[128,512]{1,0:T(8,128)(2,1)S(1)} %get-tuple-element.43), channel_id=1, source_target_pairs={{0,4},{2,6},{4,0},{6,2},{1,5},{3,7},{5,1},{7,3},{8,12},{10,14},{12... | collective-permute-start | bytes 393224 | tf_op jit(solution)/shard_map/ppermute | solution.py:285
  49.5 10.3 %collective-permute-start.4 = (bf16[128,512]{1,0:T(8,128)(2,1)S(1)}, bf16[128,512]{1,0:T(8,128)(2,1)S(1)}, u32[]{:S(2)}, u32[]{:S(2)}) collective-permute-start(bf16[128,512]{1,0:T(8,128)(2,1)S(1)} %get-tuple-element.44), channel_id=1, source_target_pairs={{0,6},{2,4},{4,2},{6,0},{1,7},{3,5},{5,3},{7,1},{8,14},{10,12},{12... | collective-permute-start | bytes 393224 | tf_op jit(solution)/shard_map/ppermute | solution.py:285
  60.0 3.9 %collective-permute-start.8 = (bf16[128,512]{1,0:T(8,128)(2,1)S(1)}, bf16[128,512]{1,0:T(8,128)(2,1)S(1)}, u32[]{:S(2)}, u32[]{:S(2)}) collective-permute-start(bf16[128,512]{1,0:T(8,128)(2,1)S(1)} %shard_map.80), channel_id=1, source_target_pairs={{0,8},{8,0},{16,24},{24,16},{1,9},{9,1},{17,25},{25,17},{2,10},{10... | collective-permute-start | bytes 393224 | tf_op jit(solution)/shard_map/ppermute | solution.py:285
  60.3 5.2 %collective-permute-start.9 = (bf16[128,512]{1,0:T(8,128)(2,1)S(1)}, bf16[128,512]{1,0:T(8,128)(2,1)S(1)}, u32[]{:S(2)}, u32[]{:S(2)}) collective-permute-start(bf16[128,512]{1,0:T(8,128)(2,1)S(1)} %shard_map.80), channel_id=1, source_target_pairs={{0,16},{8,24},{16,0},{24,8},{1,17},{9,25},{17,1},{25,9},{2,18},{10... | collective-permute-start | bytes 393224 | tf_op jit(solution)/shard_map/ppermute | solution.py:285
  60.5 5.3 %collective-permute-start.10 = (bf16[128,512]{1,0:T(8,128)(2,1)S(1)}, bf16[128,512]{1,0:T(8,128)(2,1)S(1)}, u32[]{:S(2)}, u32[]{:S(2)}) collective-permute-start(bf16[128,512]{1,0:T(8,128)(2,1)S(1)} %shard_map.80), channel_id=1, source_target_pairs={{0,24},{8,16},{16,8},{24,0},{1,25},{9,17},{17,9},{25,1},{2,26},{10... | collective-permute-start | bytes 393224 | tf_op jit(solution)/shard_map/ppermute | solution.py:285
  66.2 9.7 %collective-permute-start.14 = (bf16[128,512]{1,0:T(8,128)(2,1)S(1)}, bf16[128,512]{1,0:T(8,128)(2,1)S(1)}, u32[]{:S(2)}, u32[]{:S(2)}) collective-permute-start(bf16[128,512]{1,0:T(8,128)(2,1)S(1)} %get-tuple-element.53), channel_id=1, source_target_pairs={{0,2},{2,0},{4,6},{6,4},{1,3},{3,1},{5,7},{7,5},{8,10},{10,8},{12,... | collective-permute-start | bytes 393224 | tf_op jit(solution)/shard_map/ppermute | solution.py:285
  69.8 6.4 %collective-permute-start.15 = (bf16[128,512]{1,0:T(8,128)(2,1)S(1)}, bf16[128,512]{1,0:T(8,128)(2,1)S(1)}, u32[]{:S(2)}, u32[]{:S(2)}) collective-permute-start(bf16[128,512]{1,0:T(8,128)(2,1)S(1)} %get-tuple-element.54), channel_id=1, source_target_pairs={{0,4},{2,6},{4,0},{6,2},{1,5},{3,7},{5,1},{7,3},{8,12},{10,14},{12... | collective-permute-start | bytes 393224 | tf_op jit(solution)/shard_map/ppermute | solution.py:285
  70.9 7.5 %collective-permute-start.16 = (bf16[128,512]{1,0:T(8,128)(2,1)S(1)}, bf16[128,512]{1,0:T(8,128)(2,1)S(1)}, u32[]{:S(2)}, u32[]{:S(2)}) collective-permute-start(bf16[128,512]{1,0:T(8,128)(2,1)S(1)} %get-tuple-element.55), channel_id=1, source_target_pairs={{0,6},{2,4},{4,2},{6,0},{1,7},{3,5},{5,3},{7,1},{8,14},{10,12},{12... | collective-permute-start | bytes 393224 | tf_op jit(solution)/shard_map/ppermute | solution.py:285
  79.0 7.2 %collective-permute-start.21 = (bf16[512,512]{1,0:T(8,128)(2,1)S(1)}, bf16[512,512]{1,0:T(8,128)(2,1)S(1)}, u32[]{:S(2)}, u32[]{:S(2)}) collective-permute-start(bf16[512,512]{1,0:T(8,128)(2,1)S(1)} %get-tuple-element.63), channel_id=1, source_target_pairs={{0,1},{1,0},{2,3},{3,2},{4,5},{5,4},{6,7},{7,6},{8,9},{9,8},{10,11... | collective-permute-start | bytes 1572872 | tf_op jit(solution)/shard_map/ppermute | solution.py:285
